TPU v7x, 32 devices: a whole 2x2x4 slice. The times are simulated.
32 devices in a mesh: groups: 2 (over y), seq: 4 (over z), head: 4 (over x, core).
Axes of the slice: x: 2, y: 2, z: 4, core: 2. Of those that a mesh axis runs over, the one named last changes fastest.
Arguments:
- query: bfloat16 [8192, 1536], P(('groups', 'seq', 'head')), parts along dimension 0, may hold values from -150 to 150
- key_in: bfloat16 [8192, 1536], P(('groups', 'seq', 'head')), parts along dimension 0, may hold values from -6 to 6
- value: bfloat16 [8192, 1536], P(('groups', 'seq', 'head')), parts along dimension 0, may hold values from -6 to 6
- grad_out: bfloat16 [8192, 1536], P(('groups', 'seq', 'head')), parts along dimension 0, may hold values from -6 to 6
- pattern: int32 [16, 3], replicated, may hold values from 0 to 15, as said below
- live: int32 [16, 3], replicated, may hold values from 0 to 1, as said below
Outputs:
- attended: bfloat16 [8192, 1536], P(('groups', 'seq', 'head')), parts along dimension 0
- query_grad: bfloat16 [8192, 1536], P(('groups', 'seq', 'head')), parts along dimension 0
- key_grad: bfloat16 [8192, 1536], P(('groups', 'seq', 'head')), parts along dimension 0
- value_grad: bfloat16 [8192, 1536], P(('groups', 'seq', 'head')), parts along dimension 0
There are 2 independent parts, one for each index of `groups`. A program takes and returns all parts, laid end to end along the dimension named above; an argument that names none is the same for every part. Nothing has to cross between parts.
Inputs may be any that keep to these rules, and one draw needn't show every extreme that they name: `pattern`: each entry names a tile of the same frame-tile layer as its query tile or of the layer just before or after it; the live entries of a row are distinct; an entry that is not live names the query tile itself. Slot 0 of every row is live and names the query tile itself.
All inputs are finite; a program needn't handle non-finite values.
Results may differ from a plain program's by a relative error of at most 0.015.
Values may be sent and summed in bfloat16 or wider, within the bound.
A program may use at most 128 MiB of HBM per device.

v0:
```python
import jax
import jax.numpy as jnp
from jax import lax
from jax.sharding import PartitionSpec as P

HEADS = 12
HEAD_DIM = 128


def extended_2(cells, sides, width):
    for axis, dim in sides:
        count = lax.axis_size(axis)
        ends = count - 1
        head = lax.slice_in_dim(cells, 0, width, axis=dim)
        tail = lax.slice_in_dim(cells, cells.shape[dim] - width, cells.shape[dim], axis=dim)
        cells = jnp.concatenate(
            [
                lax.ppermute(tail, axis, [(i, (i + 1) % count) for i in range(ends)]),
                cells,
                lax.ppermute(head, axis, [((i + 1) % count, i) for i in range(ends)]),
            ],
            axis=dim,
        )
    return cells


def shifted(value, axis, steps):
    count = lax.axis_size(axis)
    initial, last = (max(0, -steps), min(count, count - steps))
    return lax.ppermute(value, axis, [(source, source + steps) for source in range(initial, last)])


def head_split(rows_flat, tiles, heads):
    width = rows_flat.shape[1]
    return rows_flat.reshape(tiles, rows_flat.shape[0] // tiles, heads, width // heads).transpose(
        2, 0, 1, 3
    )


def head_join(blocks):
    heads, tiles, tile_size, head_size = blocks.shape
    return blocks.transpose(1, 2, 0, 3).reshape(tiles * tile_size, heads * head_size)


def forward_head(q_tile, g_tile, k_all, v_all, tile_ids, alive, scale):
    k_sel = k_all[tile_ids]
    v_sel = v_all[tile_ids]
    scores = jnp.einsum("aqd,ankd->aqnk", q_tile, k_sel, preferred_element_type=jnp.float32) * scale
    scores = jnp.where(alive[:, None, :, None], scores, -jnp.inf)
    peak = jnp.max(scores, axis=(2, 3), keepdims=True)
    exponent = jnp.exp(scores - peak)
    total = jnp.sum(exponent, axis=(2, 3), keepdims=True)
    weights = exponent / total
    weights_low = weights.astype(jnp.bfloat16)
    attended = jnp.einsum(
        "aqnk,ankd->aqd", weights_low, v_sel, preferred_element_type=jnp.float32
    ).astype(jnp.bfloat16)
    weight_grad = jnp.einsum("aqd,ankd->aqnk", g_tile, v_sel, preferred_element_type=jnp.float32)
    delta = jnp.sum(weights * weight_grad, axis=(2, 3), keepdims=True)
    score_grad = (weights * (weight_grad - delta) * scale).astype(jnp.bfloat16)
    query_grad = jnp.einsum(
        "aqnk,ankd->aqd", score_grad, k_sel, preferred_element_type=jnp.float32
    ).astype(jnp.bfloat16)
    onehot = (
        tile_ids[:, :, None] == jnp.arange(k_all.shape[0], dtype=jnp.int32)[None, None, :]
    ).astype(jnp.float32)
    key_slots = jnp.einsum("aqnk,aqd->ankd", score_grad, q_tile, preferred_element_type=jnp.float32)
    value_slots = jnp.einsum(
        "aqnk,aqd->ankd", weights_low, g_tile, preferred_element_type=jnp.float32
    )
    key_sums = jnp.einsum("anj,ankd->jkd", onehot, key_slots, precision=lax.Precision.HIGHEST)
    value_sums = jnp.einsum("anj,ankd->jkd", onehot, value_slots, precision=lax.Precision.HIGHEST)
    return (attended, query_grad, key_sums, value_sums)


def body(query, key_in, value, grad_out, pattern, live):
    members = lax.axis_size("head")
    heads = HEADS // members
    scale = HEAD_DIM ** (-0.5)
    queries, keys, values, out_grads = (
        lax.all_to_all(query, "head", split_axis=1, concat_axis=0, tiled=True),
        lax.all_to_all(key_in, "head", split_axis=1, concat_axis=0, tiled=True),
        lax.all_to_all(value, "head", split_axis=1, concat_axis=0, tiled=True),
        lax.all_to_all(grad_out, "head", split_axis=1, concat_axis=0, tiled=True),
    )
    tile_size = queries.shape[0] // members
    margin = members * tile_size
    seq_index = lax.axis_index("seq")
    first = seq_index * members
    extended = extended_2(jnp.stack([keys, values]), (("seq", 1),), margin)
    rows = lax.dynamic_slice_in_dim(pattern, first, members, 0)
    alive_rows = lax.dynamic_slice_in_dim(live, first, members, 0)
    tile_ids = rows - first + members
    alive = alive_rows > 0
    q_heads = head_split(queries, members, heads)
    g_heads = head_split(out_grads, members, heads)
    k_heads = head_split(extended[0], 3 * members, heads)
    v_heads = head_split(extended[1], 3 * members, heads)

    def with_partials(operands):
        return forward_head(
            operands[0], operands[1], operands[2], operands[3], tile_ids, alive, scale
        )

    attended, query_grad, key_sums, value_sums = lax.map(
        with_partials, (q_heads, g_heads, k_heads, v_heads)
    )
    grads = jnp.stack([head_join(key_sums), head_join(value_sums)])
    from_above = shifted(grads[:, :margin].astype(jnp.bfloat16), "seq", -1).astype(jnp.float32)
    from_below = shifted(grads[:, 2 * margin :].astype(jnp.bfloat16), "seq", 1).astype(jnp.float32)
    owned = grads[:, margin : 2 * margin] + from_above + from_below
    key_own = owned[0]
    value_own = owned[1]
    result = (
        lax.all_to_all(head_join(attended), "head", split_axis=0, concat_axis=1, tiled=True),
        lax.all_to_all(head_join(query_grad), "head", split_axis=0, concat_axis=1, tiled=True),
        lax.all_to_all(
            key_own.astype(jnp.bfloat16), "head", split_axis=0, concat_axis=1, tiled=True
        ),
        lax.all_to_all(
            value_own.astype(jnp.bfloat16), "head", split_axis=0, concat_axis=1, tiled=True
        ),
    )
    return (result[0], result[1], result[2], result[3])


def solution(mesh):
    placed = (
        P(("groups", "seq", "head"), None),
        P(("groups", "seq", "head"), None),
        P(("groups", "seq", "head"), None),
        P(("groups", "seq", "head"), None),
        P(),
        P(),
    )
    return jax.shard_map(
        body,
        mesh=mesh,
        in_specs=placed,
        out_specs=(
            P(("groups", "seq", "head"), None),
            P(("groups", "seq", "head"), None),
            P(("groups", "seq", "head"), None),
            P(("groups", "seq", "head"), None),
        ),
        check_vma=False,
    )
```

profile of v0, /device:TPU:1, one launch (start us, length us, event | category | flops | bytes accessed | tf_op | source)
XLA Modules:
  0.0 321.4 jit_solution(741371311791878829)
XLA Ops:
  3.0 4.3 %all-to-all-start.1 = ((bf16[256,4,384]{0,2,1:T(8,128)(2,1)}), bf16[256,4,384]{0,2,1:T(8,128)(2,1)S(1)}, u32[]{:S(2)}, u32[]{:S(2)}) async-start(bf16[256,4,384]{0,2,1:T(8,128)(2,1)} %bitcast.30), calls=%async_computation.1 | async-start | bytes 1572864 | tf_op jit(solution)/shard_map/all_to_all | solution.py:82
  8.4 9.4 %all-to-all-done.1 = bf16[256,4,384]{0,2,1:T(8,128)(2,1)S(1)} async-done(((bf16[256,4,384]{0,2,1:T(8,128)(2,1)}), bf16[256,4,384]{0,2,1:T(8,128)(2,1)S(1)}, u32[]{:S(2)}, u32[]{:S(2)}) %all-to-all-start.1) | async-done | bytes 786464 | tf_op jit(solution)/shard_map/all_to_all | solution.py:82
  17.8 4.5 %all-to-all-start.2 = ((bf16[256,4,384]{0,2,1:T(8,128)(2,1)}), bf16[256,4,384]{0,2,1:T(8,128)(2,1)S(1)}, u32[]{:S(2)}, u32[]{:S(2)}) async-start(bf16[256,4,384]{0,2,1:T(8,128)(2,1)} %bitcast.33), calls=%async_computation.2 | async-start | bytes 1572864 | tf_op jit(solution)/shard_map/all_to_all | solution.py:83
  22.8 10.4 %all-to-all-done.2 = bf16[256,4,384]{0,2,1:T(8,128)(2,1)S(1)} async-done(((bf16[256,4,384]{0,2,1:T(8,128)(2,1)}), bf16[256,4,384]{0,2,1:T(8,128)(2,1)S(1)}, u32[]{:S(2)}, u32[]{:S(2)}) %all-to-all-start.2) | async-done | bytes 786464 | tf_op jit(solution)/shard_map/all_to_all | solution.py:83
  36.2 5.7 %collective-permute-start = (bf16[2,1024,384]{2,1,0:T(8,128)(2,1)}, bf16[2,1024,384]{2,1,0:T(8,128)(2,1)}, u32[]{:S(2)}, u32[]{:S(2)}) collective-permute-start(bf16[2,1024,384]{2,1,0:T(8,128)(2,1)} %pad_maximum_fusion.1), channel_id=1, source_target_pairs={{0,4},{4,8},{8,12},{1,5},{5,9},{9,13},{2,6},{6,10},{10,14},{3,7},{... | collective-permute-start | bytes 4718600 | tf_op jit(solution)/shard_map/ppermute | solution.py:18
  43.1 4.6 %all-to-all-start = ((bf16[256,4,384]{0,2,1:T(8,128)(2,1)}), bf16[256,4,384]{0,2,1:T(8,128)(2,1)S(1)}, u32[]{:S(2)}, u32[]{:S(2)}) async-start(bf16[256,4,384]{0,2,1:T(8,128)(2,1)} %bitcast.26), calls=%async_computation | async-start | bytes 1572864 | tf_op jit(solution)/shard_map/all_to_all | solution.py:81
  49.1 23.9 %collective-permute-done.1 = bf16[2,1024,384]{2,1,0:T(8,128)(2,1)} collective-permute-done((bf16[2,1024,384]{2,1,0:T(8,128)(2,1)}, bf16[2,1024,384]{2,1,0:T(8,128)(2,1)}, u32[]{:S(2)}, u32[]{:S(2)}) %collective-permute-start.1) | collective-permute-done | bytes 1572896 | tf_op jit(solution)/shard_map/ppermute | solution.py:20
  73.9 4.6 %pad_maximum_fusion = bf16[2,3072,384]{2,1,0:T(8,128)(2,1)} fusion(bf16[2,1024,384]{2,1,0:T(8,128)(2,1)} %collective-permute-done.1, bf16[1,1024,384]{2,1,0:T(8,128)(2,1)S(1)} %bitcast.172, bf16[1,1024,384]{2,1,0:T(8,128)(2,1)S(1)} %bitcast.170, bf16[2,1024,384]{2,1,0:T(8,128)(2,1)} %collective-permute-done), kind=kLoop, calls=%fused_computation.47 | loop fusion | flops 18874368 | bytes 9437184 | tf_op jit(solution)/shard_map/concatenate | solution.py:16
  78.5 5.9 %all-to-all-start.3 = ((bf16[256,4,384]{0,2,1:T(8,128)(2,1)}), bf16[256,4,384]{0,2,1:T(8,128)(2,1)}, u32[]{:S(2)}, u32[]{:S(2)}) async-start(bf16[256,4,384]{0,2,1:T(8,128)(2,1)} %bitcast.38), calls=%async_computation.3 | async-start | bytes 1572864 | tf_op jit(solution)/shard_map/all_to_all | solution.py:84
  84.4 4.3 %fusion.37 = (bf16[1,3072,384]{2,1,0:T(8,128)(2,1)}, bf16[1,3072,384]{2,1,0:T(8,128)(2,1)S(1)}) fusion(bf16[2,3072,384]{2,1,0:T(8,128)(2,1)} %pad_maximum_fusion), kind=kLoop, calls=%fused_computation.59 | loop fusion | bytes 9437184 | tf_op jit(solution)/shard_map/slice | solution.py:98
  88.7 4.3 %copy.49 = bf16[1,3072,384]{1,2,0:T(8,128)(2,1)} copy(bf16[1,3072,384]{2,1,0:T(8,128)(2,1)} %get-tuple-element.128) | data formatting | bytes 4718592 | tf_op jit(solution)/shard_map/slice | solution.py:98
  93.0 5.4 %reshape_squeeze.7 = bf16[12,256,3,128]{1,0,3,2:T(8,128)(2,1)} reshape(bf16[1,3072,384]{1,2,0:T(8,128)(2,1)} %copy.49) | data formatting | bytes 4718592 | tf_op jit(solution)/shard_map/reshape;squeeze | solution.py:35
  98.4 4.8 %copy.53 = bf16[3,12,256,128]{3,2,1,0:T(8,128)(2,1)} copy(bf16[3,12,256,128]{2,1,3,0:T(8,128)(2,1)} %bitcast.167) | data formatting | bytes 4718592 | tf_op jit(solution)/shard_map/while | solution.py:105
  105.9 5.4 %reshape_squeeze.6 = bf16[12,256,3,128]{1,0,3,2:T(8,128)(2,1)} reshape(bf16[1,3072,384]{1,2,0:T(8,128)(2,1)} %copy.47) | data formatting | bytes 4718592 | tf_op jit(solution)/shard_map/reshape;squeeze | solution.py:35
  111.3 4.8 %copy.52 = bf16[3,12,256,128]{3,2,1,0:T(8,128)(2,1)} copy(bf16[3,12,256,128]{2,1,3,0:T(8,128)(2,1)} %bitcast.168) | data formatting | bytes 4718592 | tf_op jit(solution)/shard_map/while | solution.py:105
  116.1 92.5 %while.16 = (s32[]{:T(128)}, bf16[3,4,256,128]{2,3,0,1:T(8,128)(2,1)}, bf16[3,4,256,128]{2,3,0,1:T(8,128)(2,1)}, f32[3,12,256,128]{3,1,2,0:T(8,128)}, f32[3,12,2...) while((s32[]{:T(128)}, ...), condition=%wide.region_4.5_spmd, body=%wide.region_0.4_spmd.sunk | while | flops 1345845504 | bytes 75555744 | solution.py:105
  142.9 4.0 %bitcast_dynamic-update-slice_fusion.5 = f32[3,12,256,128]{3,1,2,0:T(8,128)} fusion(f32[3,12,256,128]{3,1,2,0:T(8,128)} %get-tuple-element.229, s32[]{:T(128)S(6)} %copy.106, f32[4,3,256,128]{3,2,1,0:T(8,128)S(1)} %copy-done.1, s32[4,3]{0,1:T(4,128)S(1)} %copy.96), kind=kOutput, calls=%fused_computation.9.clone.1 | convolution fusion | flops 56623248 | bytes 3670068 | tf_op jit(solution)/shard_map/while/body/eval_jaxpr/anj,ankd->jkd/dot_general | solution.py:72
  173.8 4.0 %bitcast_dynamic-update-slice_fusion.5 = f32[3,12,256,128]{3,1,2,0:T(8,128)} fusion(f32[3,12,256,128]{3,1,2,0:T(8,128)} %get-tuple-element.229, s32[]{:T(128)S(6)} %copy.106, f32[4,3,256,128]{3,2,1,0:T(8,128)S(1)} %copy-done.1, s32[4,3]{0,1:T(4,128)S(1)} %copy.96), kind=kOutput, calls=%fused_computation.9.clone.1 | convolution fusion | flops 56623248 | bytes 3670068 | tf_op jit(solution)/shard_map/while/body/eval_jaxpr/anj,ankd->jkd/dot_general | solution.py:72
  200.6 4.0 %bitcast_dynamic-update-slice_fusion.4 = f32[3,12,256,128]{3,1,2,0:T(8,128)} fusion(f32[3,12,256,128]{3,1,2,0:T(8,128)} %get-tuple-element.228, s32[]{:T(128)S(6)} %copy.106, f32[4,3,256,128]{3,2,1,0:T(8,128)S(1)} %fusion.83, s32[4,3]{0,1:T(4,128)S(1)} %copy.96), kind=kOutput, calls=%fused_computation.10.clone.1 | convolution fusion | flops 56623248 | bytes 3670068 | tf_op jit(solution)/shard_map/while/body/eval_jaxpr/anj,ankd->jkd/dot_general | solution.py:71
  204.6 4.0 %bitcast_dynamic-update-slice_fusion.5 = f32[3,12,256,128]{3,1,2,0:T(8,128)} fusion(f32[3,12,256,128]{3,1,2,0:T(8,128)} %get-tuple-element.229, s32[]{:T(128)S(6)} %copy.106, f32[4,3,256,128]{3,2,1,0:T(8,128)S(1)} %copy-done.1, s32[4,3]{0,1:T(4,128)S(1)} %copy.96), kind=kOutput, calls=%fused_computation.9.clone.1 | convolution fusion | flops 56623248 | bytes 3670068 | tf_op jit(solution)/shard_map/while/body/eval_jaxpr/anj,ankd->jkd/dot_general | solution.py:72
  208.6 6.8 %copy.58 = f32[12,256,3,128]{1,0,3,2:T(8,128)} copy(f32[12,256,3,128]{3,0,1,2:T(8,128)} %bitcast.173) | data formatting | bytes 9437184 | tf_op jit(solution)/shard_map/transpose | solution.py:42
  215.4 6.9 %stack_reshape.7 = f32[1,3072,384]{1,2,0:T(8,128)} reshape(f32[12,256,3,128]{1,0,3,2:T(8,128)} %copy.58) | data formatting | bytes 9437184 | tf_op jit(solution)/shard_map/stack;reshape | solution.py:108
  222.3 6.7 %copy.57 = f32[12,256,3,128]{1,0,3,2:T(8,128)} copy(f32[12,256,3,128]{3,0,1,2:T(8,128)} %bitcast.174) | data formatting | bytes 9437184 | tf_op jit(solution)/shard_map/transpose | solution.py:42
  228.9 6.9 %stack_reshape.6 = f32[1,3072,384]{1,2,0:T(8,128)} reshape(f32[12,256,3,128]{1,0,3,2:T(8,128)} %copy.57) | data formatting | bytes 9437184 | tf_op jit(solution)/shard_map/stack;reshape | solution.py:108
  246.3 5.9 %collective-permute-start.3 = (bf16[2,1024,384]{1,2,0:T(8,128)(2,1)S(1)}, bf16[2,1024,384]{1,2,0:T(8,128)(2,1)}, u32[]{:S(2)}, u32[]{:S(2)}) collective-permute-start(bf16[2,1024,384]{1,2,0:T(8,128)(2,1)S(1)} %get-tuple-element.127), channel_id=1, source_target_pairs={{0,4},{4,8},{8,12},{1,5},{5,9},{9,13},{2,6},{6,10},{10,14},{3,7},{... | collective-permute-start | bytes 4718600 | tf_op jit(solution)/shard_map/ppermute | solution.py:30
  252.2 14.4 %all_to_all.134 = bf16[4,256,384]{1,2,0:T(8,128)(2,1)S(1)} all-to-all(bf16[4,256,384]{1,2,0:T(8,128)(2,1)S(1)} %bitcast.184), channel_id=1, replica_groups=mesh['groups'=2,'seq'=4,'head'=4] {'head'}, dimensions={0} | all-to-all | bytes 1572864 | tf_op jit(solution)/shard_map/all_to_all | solution.py:115
  266.6 4.1 %all-to-all-start.5 = ((bf16[4,256,384]{1,2,0:T(8,128)(2,1)}), bf16[4,256,384]{1,2,0:T(8,128)(2,1)S(1)}, u32[]{:S(2)}, u32[]{:S(2)}) async-start(bf16[4,256,384]{1,2,0:T(8,128)(2,1)} %bitcast.183), calls=%async_computation.5 | async-start | bytes 1572864 | tf_op jit(solution)/shard_map/all_to_all | solution.py:116
  270.7 13.5 %collective-permute-done.2 = bf16[2,1024,384]{1,2,0:T(8,128)(2,1)} collective-permute-done((bf16[2,1024,384]{1,2,0:T(8,128)(2,1)}, bf16[2,1024,384]{1,2,0:T(8,128)(2,1)}, u32[]{:S(2)}, u32[]{:S(2)}) %collective-permute-start.2) | collective-permute-done | bytes 1572896 | tf_op jit(solution)/shard_map/ppermute | solution.py:30
  289.8 4.3 %all-to-all-start.7 = ((bf16[4,256,384]{2,1,0:T(8,128)(2,1)}), bf16[4,256,384]{2,1,0:T(8,128)(2,1)S(1)}, u32[]{:S(2)}, u32[]{:S(2)}) async-start(bf16[4,256,384]{2,1,0:T(8,128)(2,1)} %bitcast.55), calls=%async_computation.7 | async-start | bytes 1572864 | tf_op jit(solution)/shard_map/all_to_all | solution.py:120
  295.2 9.6 %all-to-all-done.7 = bf16[4,256,384]{2,1,0:T(8,128)(2,1)S(1)} async-done(((bf16[4,256,384]{2,1,0:T(8,128)(2,1)}), bf16[4,256,384]{2,1,0:T(8,128)(2,1)S(1)}, u32[]{:S(2)}, u32[]{:S(2)}) %all-to-all-start.7) | async-done | bytes 786464 | tf_op jit(solution)/shard_map/all_to_all | solution.py:120
  304.9 4.3 %all-to-all-start.6 = ((bf16[4,256,384]{2,1,0:T(8,128)(2,1)}), bf16[4,256,384]{2,1,0:T(8,128)(2,1)S(1)}, u32[]{:S(2)}, u32[]{:S(2)}) async-start(bf16[4,256,384]{2,1,0:T(8,128)(2,1)} %bitcast.52), calls=%async_computation.6 | async-start | bytes 1572864 | tf_op jit(solution)/shard_map/all_to_all | solution.py:117
  313.0 7.0 %all-to-all-done.6 = bf16[4,256,384]{2,1,0:T(8,128)(2,1)S(1)} async-done(((bf16[4,256,384]{2,1,0:T(8,128)(2,1)}), bf16[4,256,384]{2,1,0:T(8,128)(2,1)S(1)}, u32[]{:S(2)}, u32[]{:S(2)}) %all-to-all-start.6) | async-done | bytes 786464 | tf_op jit(solution)/shard_map/all_to_all | solution.py:117
  (149 shorter events, 111.6 us)
Async XLA Ops:
  0.6 6.6 %copy-start.8 = (bf16[256,1536]{1,0:T(8,128)(2,1)S(1)}, bf16[256,1536]{1,0:T(8,128)(2,1)}, u32[]{:S(2)}) copy-start(bf16[256,1536]{1,0:T(8,128)(2,1)} %param.10) | copy-start | bytes 2359300
  3.0 14.8 %all-to-all-start.1 = ((bf16[256,4,384]{0,2,1:T(8,128)(2,1)}), bf16[256,4,384]{0,2,1:T(8,128)(2,1)S(1)}, u32[]{:S(2)}, u32[]{:S(2)}) async-start(bf16[256,4,384]{0,2,1:T(8,128)(2,1)} %bitcast.30), calls=%async_computation.1 | async-start | bytes 1572864 | tf_op jit(solution)/shard_map/all_to_all | solution.py:82
  17.8 15.3 %all-to-all-start.2 = ((bf16[256,4,384]{0,2,1:T(8,128)(2,1)}), bf16[256,4,384]{0,2,1:T(8,128)(2,1)S(1)}, u32[]{:S(2)}, u32[]{:S(2)}) async-start(bf16[256,4,384]{0,2,1:T(8,128)(2,1)} %bitcast.33), calls=%async_computation.2 | async-start | bytes 1572864 | tf_op jit(solution)/shard_map/all_to_all | solution.py:83
  22.7 19.2 %copy-start.9 = (bf16[256,1536]{1,0:T(8,128)(2,1)S(1)}, bf16[256,1536]{1,0:T(8,128)(2,1)}, u32[]{:S(2)}) copy-start(bf16[256,1536]{1,0:T(8,128)(2,1)} %param.8) | copy-start | bytes 2359300
  33.5 14.1 %copy-start.12 = (s32[16,3]{0,1:T(4,128)S(1)}, s32[16,3]{0,1:T(4,128)}, u32[]{:S(2)}) copy-start(s32[16,3]{0,1:T(4,128)} %param.12) | copy-start | bytes 580
  33.5 14.1 %copy-start.13 = (s32[16,3]{0,1:T(4,128)S(1)}, s32[16,3]{0,1:T(4,128)}, u32[]{:S(2)}) copy-start(s32[16,3]{0,1:T(4,128)} %param.13) | copy-start | bytes 580
  33.6 14.4 %copy-start.10 = (bf16[256,1536]{1,0:T(8,128)(2,1)S(1)}, bf16[256,1536]{1,0:T(8,128)(2,1)}, u32[]{:S(2)}) copy-start(bf16[256,1536]{1,0:T(8,128)(2,1)} %param.11) | copy-start | bytes 2359300
  34.9 38.1 %collective-permute-start.1 = (bf16[2,1024,384]{2,1,0:T(8,128)(2,1)}, bf16[2,1024,384]{2,1,0:T(8,128)(2,1)}, u32[]{:S(2)}, u32[]{:S(2)}) collective-permute-start(bf16[2,1024,384]{2,1,0:T(8,128)(2,1)} %pad_maximum_fusion.1), channel_id=1, source_target_pairs={{4,0},{8,4},{12,8},{5,1},{9,5},{13,9},{6,2},{10,6},{14,10},{7,3},{... | collective-permute-start | bytes 4718600 | tf_op jit(solution)/shard_map/ppermute | solution.py:20
  36.2 37.7 %collective-permute-start = (bf16[2,1024,384]{2,1,0:T(8,128)(2,1)}, bf16[2,1024,384]{2,1,0:T(8,128)(2,1)}, u32[]{:S(2)}, u32[]{:S(2)}) collective-permute-start(bf16[2,1024,384]{2,1,0:T(8,128)(2,1)} %pad_maximum_fusion.1), channel_id=1, source_target_pairs={{0,4},{4,8},{8,12},{1,5},{5,9},{9,13},{2,6},{6,10},{10,14},{3,7},{... | collective-permute-start | bytes 4718600 | tf_op jit(solution)/shard_map/ppermute | solution.py:18
  43.1 35.5 %all-to-all-start = ((bf16[256,4,384]{0,2,1:T(8,128)(2,1)}), bf16[256,4,384]{0,2,1:T(8,128)(2,1)S(1)}, u32[]{:S(2)}, u32[]{:S(2)}) async-start(bf16[256,4,384]{0,2,1:T(8,128)(2,1)} %bitcast.26), calls=%async_computation | async-start | bytes 1572864 | tf_op jit(solution)/shard_map/all_to_all | solution.py:81
  78.5 37.6 %all-to-all-start.3 = ((bf16[256,4,384]{0,2,1:T(8,128)(2,1)}), bf16[256,4,384]{0,2,1:T(8,128)(2,1)}, u32[]{:S(2)}, u32[]{:S(2)}) async-start(bf16[256,4,384]{0,2,1:T(8,128)(2,1)} %bitcast.38), calls=%async_computation.3 | async-start | bytes 1572864 | tf_op jit(solution)/shard_map/all_to_all | solution.py:84
  121.6 2.6 copy-start.3
  128.0 3.0 copy-start.4
  133.0 1.1 copy-start
  136.4 6.5 %copy-start.1 = (f32[4,3,256,128]{3,2,1,0:T(8,128)S(1)}, f32[4,3,256,128]{3,2,1,0:T(8,128)}, u32[]{:S(2)}) copy-start(f32[4,3,256,128]{3,2,1,0:T(8,128)} %fusion.84) | copy-start | bytes 4718596 | tf_op jit(solution)/shard_map/while
  142.9 4.0 %copy-start.7 = (bf16[3,4,256,128]{2,3,0,1:T(8,128)(2,1)S(1)}, bf16[3,4,256,128]{2,3,0,1:T(8,128)(2,1)}, u32[]{:S(2)}) copy-start(bf16[3,4,256,128]{2,3,0,1:T(8,128)(2,1)} %copy-done.6) | copy-start | bytes 2359300 | tf_op jit(solution)/shard_map/while
  152.4 2.6 copy-start.3
  158.8 3.0 copy-start.4
  167.3 6.5 %copy-start.1 = (f32[4,3,256,128]{3,2,1,0:T(8,128)S(1)}, f32[4,3,256,128]{3,2,1,0:T(8,128)}, u32[]{:S(2)}) copy-start(f32[4,3,256,128]{3,2,1,0:T(8,128)} %fusion.84) | copy-start | bytes 4718596 | tf_op jit(solution)/shard_map/while
  173.8 4.0 %copy-start.7 = (bf16[3,4,256,128]{2,3,0,1:T(8,128)(2,1)S(1)}, bf16[3,4,256,128]{2,3,0,1:T(8,128)(2,1)}, u32[]{:S(2)}) copy-start(bf16[3,4,256,128]{2,3,0,1:T(8,128)(2,1)} %copy-done.6) | copy-start | bytes 2359300 | tf_op jit(solution)/shard_map/while
  183.3 2.6 copy-start.3
  189.6 3.0 copy-start.4
  198.1 6.6 %copy-start.1 = (f32[4,3,256,128]{3,2,1,0:T(8,128)S(1)}, f32[4,3,256,128]{3,2,1,0:T(8,128)}, u32[]{:S(2)}) copy-start(f32[4,3,256,128]{3,2,1,0:T(8,128)} %fusion.84) | copy-start | bytes 4718596 | tf_op jit(solution)/shard_map/while
  204.6 4.0 %copy-start.7 = (bf16[3,4,256,128]{2,3,0,1:T(8,128)(2,1)S(1)}, bf16[3,4,256,128]{2,3,0,1:T(8,128)(2,1)}, u32[]{:S(2)}) copy-start(bf16[3,4,256,128]{2,3,0,1:T(8,128)(2,1)} %copy-done.6) | copy-start | bytes 2359300 | tf_op jit(solution)/shard_map/while
  235.8 3.8 %copy-start.5 = (f32[1,3072,384]{1,2,0:T(8,128)S(1)}, f32[1,3072,384]{1,2,0:T(8,128)}, u32[]{:S(2)}) copy-start(f32[1,3072,384]{1,2,0:T(8,128)} %stack_reshape.7) | copy-start | bytes 14155780
  239.9 3.7 %copy-start.2 = (f32[2,3072,384]{1,2,0:T(8,128)}, f32[2,3072,384]{1,2,0:T(8,128)S(1)}, u32[]{:S(2)}) copy-start(f32[2,3072,384]{1,2,0:T(8,128)S(1)} %constant_dynamic-update-slice_fusion.2) | copy-start | bytes 28311556
  243.6 8.7 %copy-start.11 = (bf16[3,4,256,128]{2,3,0,1:T(8,128)(2,1)S(1)}, bf16[3,4,256,128]{2,3,0,1:T(8,128)(2,1)}, u32[]{:S(2)}) copy-start(bf16[3,4,256,128]{2,3,0,1:T(8,128)(2,1)} %get-tuple-element.64) | copy-start | bytes 2359300
  245.0 39.1 %collective-permute-start.2 = (bf16[2,1024,384]{1,2,0:T(8,128)(2,1)}, bf16[2,1024,384]{1,2,0:T(8,128)(2,1)}, u32[]{:S(2)}, u32[]{:S(2)}) collective-permute-start(bf16[2,1024,384]{1,2,0:T(8,128)(2,1)} %get-tuple-element.126), channel_id=1, source_target_pairs={{4,0},{8,4},{12,8},{5,1},{9,5},{13,9},{6,2},{10,6},{14,10},{7,3},{... | collective-permute-start | bytes 4718600 | tf_op jit(solution)/shard_map/ppermute | solution.py:30
  246.3 38.5 %collective-permute-start.3 = (bf16[2,1024,384]{1,2,0:T(8,128)(2,1)S(1)}, bf16[2,1024,384]{1,2,0:T(8,128)(2,1)}, u32[]{:S(2)}, u32[]{:S(2)}) collective-permute-start(bf16[2,1024,384]{1,2,0:T(8,128)(2,1)S(1)} %get-tuple-element.127), channel_id=1, source_target_pairs={{0,4},{4,8},{8,12},{1,5},{5,9},{9,13},{2,6},{6,10},{10,14},{3,7},{... | collective-permute-start | bytes 4718600 | tf_op jit(solution)/shard_map/ppermute | solution.py:30
  266.6 23.2 %all-to-all-start.5 = ((bf16[4,256,384]{1,2,0:T(8,128)(2,1)}), bf16[4,256,384]{1,2,0:T(8,128)(2,1)S(1)}, u32[]{:S(2)}, u32[]{:S(2)}) async-start(bf16[4,256,384]{1,2,0:T(8,128)(2,1)} %bitcast.183), calls=%async_computation.5 | async-start | bytes 1572864 | tf_op jit(solution)/shard_map/all_to_all | solution.py:116
  289.8 15.1 %all-to-all-start.7 = ((bf16[4,256,384]{2,1,0:T(8,128)(2,1)}), bf16[4,256,384]{2,1,0:T(8,128)(2,1)S(1)}, u32[]{:S(2)}, u32[]{:S(2)}) async-start(bf16[4,256,384]{2,1,0:T(8,128)(2,1)} %bitcast.55), calls=%async_computation.7 | async-start | bytes 1572864 | tf_op jit(solution)/shard_map/all_to_all | solution.py:120
  304.9 15.1 %all-to-all-start.6 = ((bf16[4,256,384]{2,1,0:T(8,128)(2,1)}), bf16[4,256,384]{2,1,0:T(8,128)(2,1)S(1)}, u32[]{:S(2)}, u32[]{:S(2)}) async-start(bf16[4,256,384]{2,1,0:T(8,128)(2,1)} %bitcast.52), calls=%async_computation.6 | async-start | bytes 1572864 | tf_op jit(solution)/shard_map/all_to_all | solution.py:117
  (5 other events, 5.0 us)
where the time goes:
time: 326 us; the launch traced here: 321 us
  local copies, waits for them, and re-layouts  111 us (34%)
  waiting for transfers between devices  75.4 us (23%)
  matrix products  57.4 us (18%)
  starting transfers between devices  46.2 us (14%)
  other arithmetic  15.9 us (5%)
  blocking collectives  14.4 us (4%)
    ppermute x1, waiting for transfers between devices, extended_2(): lax.ppermute(head, axis, [((i + 1) % count, i) for i in range(ends)])  23.9 us
    unnamed x27, local copies, waits for them, and re-layouts  17.3 us
    all_to_all x1, blocking collectives, body(): lax.all_to_all(head_join(attended), 'head', split_axis=0, concat_axis=1,...  14.4 us
    ppermute x2, waiting for transfers between devices, shifted(): lax.ppermute(value, axis, [(source, source + steps) for source in range(i...  14.1 us
    another operation x3, local copies, waits for them, and re-layouts, body(): grads = jnp.stack([head_join(key_sums), head_join(value_sums)])  14 us
    transpose x2, local copies, waits for them, and re-layouts, head_join(): blocks.transpose(1, 2, 0, 3).reshape(tiles * tile_size, heads * head_size)  13.5 us
    dynamic_update_slice x12, local copies, waits for them, and re-layouts, body(): lax.map(with_partials, (q_heads, g_heads, k_heads, v_heads))  13 us
    dot_general x3, matrix products, forward_head(): jnp.einsum('anj,ankd->jkd', onehot, value_slots, precision=lax.Precision....  12.1 us
  transfers between devices with their start and end apart: 11, of which 8 were waited for; matrix products, arithmetic and copies ran while one was open for 16% of the time, Pallas kernels for 0%

commit v1 on v0

v1 whole, which is shorter than its diff:
```python
import functools

import jax
import jax.numpy as jnp
from jax import lax
from jax.experimental import pallas as pl
from jax.experimental.pallas import tpu as pltpu
from jax.sharding import PartitionSpec as P

HEADS = 12
HEAD_DIM = 128
MESH = pl.DeviceIdType.MESH
NT = (((1,), (1,)), ((), ()))
NN = (((1,), (0,)), ((), ()))
TN = (((0,), (0,)), ((), ()))


def dot(a, b, dims):
    return lax.dot_general(a, b, dims, preferred_element_type=jnp.float32)


def kernel(
    members, layers, pattern, live, query, key_in, value, grad_out,
    att_out, dq_out, dk_out, dv_out,
    qg, res, slots, own, gsend, grecv, total,
    xin_send, xin_recv, xin_local, z_send, z_recv, zb_send, zb_recv,
    xb_send, xb_recv, xb_local, *kv,
):
    me = lax.axis_index("head")
    seq = lax.axis_index("seq")
    heads = HEADS // members
    nb = pattern.shape[1]
    first = seq * members
    scale = HEAD_DIM ** (-0.5)
    has_below = seq > 0
    has_above = seq < layers - 1
    below = jnp.maximum(seq - 1, 0)
    above = jnp.minimum(seq + 1, layers - 1)
    partners = [lax.rem(me + off, members) for off in range(1, members)]

    def columns(owner, h):
        return pl.ds(pl.multiple_of((owner * heads + h) * HEAD_DIM, HEAD_DIM), HEAD_DIM)

    barrier = pltpu.get_barrier_semaphore()
    for p in partners:
        pl.semaphore_signal(barrier, inc=1, device_id={"head": p}, device_id_type=MESH)

    @pl.when(has_below)
    def _():
        pl.semaphore_signal(barrier, inc=1, device_id={"seq": below}, device_id_type=MESH)

    @pl.when(has_above)
    def _():
        pl.semaphore_signal(barrier, inc=1, device_id={"seq": above}, device_id_type=MESH)

    pl.semaphore_wait(
        barrier, members - 1 + has_below.astype(jnp.int32) + has_above.astype(jnp.int32)
    )

    sources = (key_in, value, query, grad_out)

    def landing(h, arr, tile):
        if arr < 2:
            return kv[h].at[members + tile, arr]
        return qg.at[h, tile, arr - 2]

    def x_in(h, arr, off):
        return pltpu.make_async_remote_copy(
            src_ref=sources[arr].at[:, columns(partners[off], h)],
            dst_ref=landing(h, arr, me),
            send_sem=xin_send.at[h, arr, off],
            recv_sem=xin_recv.at[h, arr, off],
            device_id={"head": partners[off]},
            device_id_type=MESH,
        )

    def x_own(h, arr):
        return pltpu.make_async_copy(
            sources[arr].at[:, columns(me, h)], landing(h, arr, me), xin_local.at[h, arr]
        )

    def x_in_wait(h, arrs):
        for arr in arrs:
            x_own(h, arr).wait()
            for off in range(members - 1):
                x_in(h, arr, off).wait_recv()

    def z_in(h, up):
        return pltpu.make_async_remote_copy(
            src_ref=kv[h].at[pl.ds(members, members)],
            dst_ref=kv[h].at[pl.ds(0 if up else 2 * members, members)],
            send_sem=z_send.at[h, up],
            recv_sem=z_recv.at[h, up],
            device_id={"seq": above if up else below},
            device_id_type=MESH,
        )

    def z_back(h, up):
        return pltpu.make_async_remote_copy(
            src_ref=gsend.at[h, up],
            dst_ref=grecv.at[h, up],
            send_sem=zb_send.at[h, up],
            recv_sem=zb_recv.at[h, up],
            device_id={"seq": above if up else below},
            device_id_type=MESH,
        )

    def z_start(make, h):
        for up, there in ((1, has_above), (0, has_below)):
            @pl.when(there)
            def _():
                make(h, up).start()

    def z_wait_recv(make, h):
        for up, there in ((1, has_below), (0, has_above)):
            @pl.when(there)
            def _():
                make(h, up).wait_recv()

    def z_wait_send(make, h):
        for up, there in ((1, has_above), (0, has_below)):
            @pl.when(there)
            def _():
                make(h, up).wait_send()

    results = (dk_out, dv_out, att_out, dq_out)

    def outgoing(h, arr, tile):
        if arr < 2:
            return total.at[h, tile, arr]
        return res.at[h, tile, arr - 2]

    def x_back(h, arr, off):
        return pltpu.make_async_remote_copy(
            src_ref=outgoing(h, arr, partners[off]),
            dst_ref=results[arr].at[:, columns(me, h)],
            send_sem=xb_send.at[h, arr, off],
            recv_sem=xb_recv.at[h, arr, off],
            device_id={"head": partners[off]},
            device_id_type=MESH,
        )

    def x_back_own(h, arr):
        return pltpu.make_async_copy(
            outgoing(h, arr, me), results[arr].at[:, columns(me, h)], xb_local.at[h, arr]
        )

    def x_back_start(h, arrs):
        for arr in arrs:
            for off in range(members - 1):
                x_back(h, arr, off).start()
            x_back_own(h, arr).start()

    def attend(h):
        def tile_step(a, carry):
            row = first + a
            ids = [
                jnp.clip(pattern[row, n] - first + members, 0, 3 * members - 1) for n in range(nb)
            ]
            bias = [jnp.where(live[row, n] > 0, 0.0, -jnp.inf) for n in range(nb)]
            q = qg[h, a, 0]
            g = qg[h, a, 1]
            scores = [dot(q, kv[h][ids[n], 0], NT) * scale + bias[n] for n in range(nb)]
            peak = functools.reduce(
                jnp.maximum, [jnp.max(s, axis=1, keepdims=True) for s in scores]
            )
            exps = [jnp.exp(s - peak) for s in scores]
            norm = 1.0 / sum(jnp.sum(e, axis=1, keepdims=True) for e in exps)
            weights = [e * norm for e in exps]
            low = [w.astype(jnp.bfloat16) for w in weights]
            res[h, a, 0] = sum(dot(low[n], kv[h][ids[n], 1], NN) for n in range(nb)).astype(
                jnp.bfloat16
            )
            wgrad = [dot(g, kv[h][ids[n], 1], NT) for n in range(nb)]
            delta = sum(
                jnp.sum(weights[n] * wgrad[n], axis=1, keepdims=True) for n in range(nb)
            )
            sgrad = [
                (weights[n] * (wgrad[n] - delta) * scale).astype(jnp.bfloat16)
                for n in range(nb)
            ]
            res[h, a, 1] = sum(dot(sgrad[n], kv[h][ids[n], 0], NN) for n in range(nb)).astype(
                jnp.bfloat16
            )
            for n in range(nb):
                slots[a * nb + n, 0] = dot(sgrad[n], q, TN)
                slots[a * nb + n, 1] = dot(low[n], g, TN)
            return carry

        lax.fori_loop(0, members, tile_step, 0)

    def gather_slots(j, which):
        terms = []
        for a in range(members):
            row = first + a
            index = jnp.int32(members * nb)
            for n in range(nb):
                hit = (pattern[row, n] - first + members == j) & (live[row, n] > 0)
                index = jnp.where(hit, a * nb + n, index)
            terms.append(index)
        return sum(slots[index, which] for index in terms)

    def spread(h):
        def outer(j, carry):
            for which in range(2):
                gsend[h, 0, j, which] = gather_slots(j, which).astype(jnp.bfloat16)
                gsend[h, 1, j, which] = gather_slots(j + 2 * members, which).astype(jnp.bfloat16)
            return carry

        lax.fori_loop(0, members, outer, 0)
        z_start(z_back, h)

        def inner(j, carry):
            for which in range(2):
                own[h, j, which] = gather_slots(j + members, which)
            return carry

        lax.fori_loop(0, members, inner, 0)

    def finish(h):
        z_wait_recv(z_back, h)

        @pl.when(has_below)
        def _():
            own[h] += grecv[h, 1].astype(jnp.float32)

        @pl.when(has_above)
        def _():
            own[h] += grecv[h, 0].astype(jnp.float32)

        total[h] = own[h].astype(jnp.bfloat16)
        x_back_start(h, (0, 1))

    for h in range(heads):
        for arr in range(4):
            for off in range(members - 1):
                x_in(h, arr, off).start()
            x_own(h, arr).start()

    slots[members * nb] = jnp.zeros(slots.shape[1:], slots.dtype)

    def feed(h):
        x_in_wait(h, (0, 1))
        z_start(z_in, h)

    feed(0)
    for h in range(heads):
        if h + 1 < heads:
            feed(h + 1)
        x_in_wait(h, (2, 3))
        z_wait_recv(z_in, h)
        attend(h)
        x_back_start(h, (2, 3))
        spread(h)
        if h >= 2:
            finish(h - 2)
    for h in range(max(heads - 2, 0), heads):
        finish(h)

    for h in range(heads):
        z_wait_send(z_in, h)
        z_wait_send(z_back, h)
        for arr in range(4):
            x_back_own(h, arr).wait()
            for off in range(members - 1):
                x_in(h, arr, off).wait_send()
                x_back(h, arr, off).wait_send()
                x_back(h, arr, off).wait_recv()


def body(members, layers, query, key_in, value, grad_out, pattern, live):
    tile = query.shape[0]
    heads = HEADS // members
    nb = pattern.shape[1]
    dma = pltpu.SemaphoreType.DMA
    bf16 = jnp.bfloat16
    block = (tile, HEAD_DIM)
    return pl.pallas_call(
        functools.partial(kernel, members, layers),
        out_shape=[jax.ShapeDtypeStruct(query.shape, bf16)] * 4,
        in_specs=[pl.BlockSpec(memory_space=pltpu.SMEM)] * 2
        + [pl.BlockSpec(memory_space=pl.ANY)] * 4,
        out_specs=[pl.BlockSpec(memory_space=pl.ANY)] * 4,
        scratch_shapes=[
            pltpu.VMEM((heads, members, 2) + block, bf16),
            pltpu.VMEM((heads, members, 2) + block, bf16),
            pltpu.VMEM((members * nb + 1, 2) + block, jnp.float32),
            pltpu.VMEM((heads, members, 2) + block, jnp.float32),
            pltpu.VMEM((heads, 2, members, 2) + block, bf16),
            pltpu.VMEM((heads, 2, members, 2) + block, bf16),
            pltpu.VMEM((heads, members, 2) + block, bf16),
            dma((heads, 4, members - 1)),
            dma((heads, 4, members - 1)),
            dma((heads, 4)),
            dma((heads, 2)),
            dma((heads, 2)),
            dma((heads, 2)),
            dma((heads, 2)),
            dma((heads, 4, members - 1)),
            dma((heads, 4, members - 1)),
            dma((heads, 4)),
        ]
        + [pltpu.VMEM((3 * members, 2) + block, bf16)] * heads,
        compiler_params=pltpu.CompilerParams(collective_id=0, has_side_effects=True),
    )(pattern, live, query, key_in, value, grad_out)


def solution(mesh):
    rows = P(("groups", "seq", "head"), None)
    return jax.shard_map(
        functools.partial(body, mesh.shape["head"], mesh.shape["seq"]),
        mesh=mesh,
        in_specs=(rows, rows, rows, rows, P(), P()),
        out_specs=(rows, rows, rows, rows),
        check_vma=False,
    )
```

time: 326 us -> 99 us (0.30); the launches traced: 321 us -> 98.7 us
  local copies, waits for them, and re-layouts: 111 us -> 7.9 us
  Pallas kernels: 0 us -> 90.1 us
  waiting for transfers between devices: 75.4 us -> 0 us
  matrix products: 57.4 us -> 0 us
  starting transfers between devices: 46.2 us -> 0 us
  other arithmetic: 15.9 us -> 0 us
  blocking collectives: 14.4 us -> 0 us
    pallas_call x0 -> x1, Pallas kernels: none -> 90.1 us  [body(): pl.pallas_call(functools.partial(kernel, members, layers), out_shape=[jax...]
    dot_general x24 -> x0, matrix products: 57.4 us -> none  [the longest x3 12.1 us: forward_head(): jnp.einsum('anj,ankd->jkd', onehot, value_slots, precision=lax.Precision....]
    ppermute x4 -> x0, waiting for transfers between devices: 38.9 us -> none  [the longest x1 23.9 us: extended_2(): lax.ppermute(head, axis, [((i + 1) % count, i) for i in range(ends)])]
    all_to_all x7 -> x0, waiting for transfers between devices: 36.5 us -> none  [the longest x1 10.4 us: body(): lax.all_to_all(value, 'head', split_axis=1, concat_axis=0, tiled=True)]
    all_to_all x7 -> x0, starting transfers between devices: 32.1 us -> none  [the longest x1 5.91 us: body(): lax.all_to_all(grad_out, 'head', split_axis=1, concat_axis=0, tiled=True)]
    another operation x8 -> x0, local copies, waits for them, and re-layouts: 25.1 us -> none  [the longest x3 14 us: body(): grads = jnp.stack([head_join(key_sums), head_join(value_sums)])]
    slice x7 -> x0, local copies, waits for them, and re-layouts: 15.1 us -> none  [the longest x2 8.53 us: body(): v_heads = head_split(extended[1], 3 * members, heads)]
    all_to_all x1 -> x0, blocking collectives: 14.4 us -> none  [body(): lax.all_to_all(head_join(attended), 'head', split_axis=0, concat_axis=1,...]
  transfers between devices with their start and end apart: 11 -> 0, of which waited for: 8 -> 0; matrix products, arithmetic and copies ran while one was open for 16% -> 0% of each run, Pallas kernels for 0% -> 0%
where the time goes in v1:
time: 99 us; the launch traced here: 98.7 us
  Pallas kernels  90.1 us (91%)
  local copies, waits for them, and re-layouts  7.9 us (8%)
    pallas_call x1, Pallas kernels, body(): pl.pallas_call(functools.partial(kernel, members, layers), out_shape=[jax...  90.1 us
    unnamed x14, local copies, waits for them, and re-layouts  7.9 us

profile of v1, /device:TPU:1, one launch (start us, length us, event | category | flops | bytes accessed | tf_op | source)
XLA Modules:
  0.0 98.7 jit_solution(15899472202832590616)
XLA Ops:
  0.6 0.0 copy-start.3
  0.6 1.4 %copy.10.pattern = s32[16,3]{1,0:T(8,128)} copy(s32[16,3]{0,1:T(4,128)} %param.10) | data formatting | bytes 384 | tf_op args[4]
  2.0 0.0 copy-done.3
  2.0 0.7 copy.11.live
  2.7 90.1 %shard_map.93 = (bf16[256,1536]{1,0:T(8,128)(2,1)}, bf16[256,1536]{1,0:T(8,128)(2,1)}, bf16[256,1536]{1,0:T(8,128)(2,1)}, bf16[256,1536]{1,0:T(8,128)(2,1)}) custom-call(s32[16,3]{1,0:T(8,128)} %copy.10.pattern, s32[16,3]{1,0:T(8,128)} %copy.11.live, bf16[256,1536]{1,0:T(8,128)(2,1)} %query.1, bf16[256,1536]{1,0:T(8,128)(2,1)} %key_in.1, ...), custom_call_target="tpu_custom_call" | custom-call | tf_op jit(solution)/shard_map/pallas_call | solution.py:278
  92.8 0.0 copy-start.2
  92.8 2.1 %copy.16 = bf16[256,1536]{1,0:T(8,128)(2,1)} copy(bf16[256,1536]{1,0:T(8,128)(2,1)} %get-tuple-element.8) | data formatting | bytes 1572864
  94.9 0.0 copy-done.2
  94.9 0.0 copy-start.1
  94.9 0.9 copy.17
  95.8 0.5 copy-done.1
  96.4 0.0 copy-start
  96.4 0.9 copy.18
  97.2 0.5 copy-done
  97.8 0.9 copy.19
Async XLA Ops:
  0.6 1.4 %copy-start.3 = (s32[16,3]{0,1:T(4,128)S(1)}, s32[16,3]{0,1:T(4,128)}, u32[]{:S(2)}) copy-start(s32[16,3]{0,1:T(4,128)} %param.11) | copy-start | bytes 580
  92.8 2.1 %copy-start.2 = (bf16[256,1536]{1,0:T(8,128)(2,1)S(1)}, bf16[256,1536]{1,0:T(8,128)(2,1)}, u32[]{:S(2)}) copy-start(bf16[256,1536]{1,0:T(8,128)(2,1)} %get-tuple-element.9) | copy-start | bytes 2359300
  94.9 1.4 %copy-start.1 = (bf16[256,1536]{1,0:T(8,128)(2,1)S(1)}, bf16[256,1536]{1,0:T(8,128)(2,1)}, u32[]{:S(2)}) copy-start(bf16[256,1536]{1,0:T(8,128)(2,1)} %get-tuple-element.10) | copy-start | bytes 2359300
  96.4 1.4 %copy-start = (bf16[256,1536]{1,0:T(8,128)(2,1)S(1)}, bf16[256,1536]{1,0:T(8,128)(2,1)}, u32[]{:S(2)}) copy-start(bf16[256,1536]{1,0:T(8,128)(2,1)} %get-tuple-element.11) | copy-start | bytes 2359300

commit v2 on v1

--- a/solution.py
+++ b/solution.py
@@ -19,24 +19,34 @@
     return lax.dot_general(a, b, dims, preferred_element_type=jnp.float32)
 
 
+def flipped(index, bits, members):
+    bit = 1
+    while bit < members:
+        if bits & bit:
+            index = index + bit * (1 - 2 * lax.rem(lax.div(index, bit), 2))
+        bit *= 2
+    return index
+
+
 def kernel(
-    members, layers, pattern, live, query, key_in, value, grad_out,
+    members, layers, pattern_in, live_in, query, key_in, value, grad_out,
     att_out, dq_out, dk_out, dv_out,
     qg, res, slots, own, gsend, grecv, total,
-    xin_send, xin_recv, xin_local, z_send, z_recv, zb_send, zb_recv,
+    pattern, live, table_sem, xin_send, xin_recv, xin_local, z_send, z_recv, zb_send, zb_recv,
     xb_send, xb_recv, xb_local, *kv,
 ):
     me = lax.axis_index("head")
     seq = lax.axis_index("seq")
     heads = HEADS // members
-    nb = pattern.shape[1]
+    nb = pattern.shape[0]
     first = seq * members
     scale = HEAD_DIM ** (-0.5)
     has_below = seq > 0
     has_above = seq < layers - 1
     below = jnp.maximum(seq - 1, 0)
     above = jnp.minimum(seq + 1, layers - 1)
-    partners = [lax.rem(me + off, members) for off in range(1, members)]
+    peers = [flipped(me, k, members) for k in range(members)]
+    partners = peers[1:]
 
     def columns(owner, h):
         return pl.ds(pl.multiple_of((owner * heads + h) * HEAD_DIM, HEAD_DIM), HEAD_DIM)
@@ -79,49 +89,54 @@
             sources[arr].at[:, columns(me, h)], landing(h, arr, me), xin_local.at[h, arr]
         )
 
-    def x_in_wait(h, arrs):
-        for arr in arrs:
-            x_own(h, arr).wait()
-            for off in range(members - 1):
-                x_in(h, arr, off).wait_recv()
-
-    def z_in(h, up):
+    def x_in_wait(h, arrs, ks):
+        for k in ks:
+            for arr in arrs:
+                if k == 0:
+                    x_own(h, arr).wait()
+                else:
+                    x_in(h, arr, k - 1).wait_recv()
+
+    def z_in(h, k, up):
         return pltpu.make_async_remote_copy(
-            src_ref=kv[h].at[pl.ds(members, members)],
-            dst_ref=kv[h].at[pl.ds(0 if up else 2 * members, members)],
-            send_sem=z_send.at[h, up],
-            recv_sem=z_recv.at[h, up],
+            src_ref=kv[h].at[members + peers[k]],
+            dst_ref=kv[h].at[peers[k] + (0 if up else 2 * members)],
+            send_sem=z_send.at[h, k, up],
+            recv_sem=z_recv.at[h, k, up],
             device_id={"seq": above if up else below},
             device_id_type=MESH,
         )
 
-    def z_back(h, up):
+    def z_back(h, k, up):
         return pltpu.make_async_remote_copy(
-            src_ref=gsend.at[h, up],
-            dst_ref=grecv.at[h, up],
-            send_sem=zb_send.at[h, up],
-            recv_sem=zb_recv.at[h, up],
+            src_ref=gsend.at[h, up, peers[k]],
+            dst_ref=grecv.at[h, up, peers[k]],
+            send_sem=zb_send.at[h, k, up],
+            recv_sem=zb_recv.at[h, k, up],
             device_id={"seq": above if up else below},
             device_id_type=MESH,
         )
 
-    def z_start(make, h):
+    def z_start(make, h, ks):
         for up, there in ((1, has_above), (0, has_below)):
             @pl.when(there)
             def _():
-                make(h, up).start()
-
-    def z_wait_recv(make, h):
+                for k in ks:
+                    make(h, k, up).start()
+
+    def z_wait_recv(make, h, ks):
         for up, there in ((1, has_below), (0, has_above)):
             @pl.when(there)
             def _():
-                make(h, up).wait_recv()
-
-    def z_wait_send(make, h):
+                for k in ks:
+                    make(h, k, up).wait_recv()
+
+    def z_wait_send(make, h, ks):
         for up, there in ((1, has_above), (0, has_below)):
             @pl.when(there)
             def _():
-                make(h, up).wait_send()
+                for k in ks:
+                    make(h, k, up).wait_send()
 
     results = (dk_out, dv_out, att_out, dq_out)
 
@@ -145,19 +160,21 @@
             outgoing(h, arr, me), results[arr].at[:, columns(me, h)], xb_local.at[h, arr]
         )
 
-    def x_back_start(h, arrs):
-        for arr in arrs:
-            for off in range(members - 1):
-                x_back(h, arr, off).start()
-            x_back_own(h, arr).start()
+    def x_back_start(h, arrs, ks):
+        for k in ks:
+            for arr in arrs:
+                if k == 0:
+                    x_back_own(h, arr).start()
+                else:
+                    x_back(h, arr, k - 1).start()
 
     def attend(h):
         def tile_step(a, carry):
             row = first + a
             ids = [
-                jnp.clip(pattern[row, n] - first + members, 0, 3 * members - 1) for n in range(nb)
+                jnp.clip(pattern[n, row] - first + members, 0, 3 * members - 1) for n in range(nb)
             ]
-            bias = [jnp.where(live[row, n] > 0, 0.0, -jnp.inf) for n in range(nb)]
+            bias = [jnp.where(live[n, row] > 0, 0.0, -jnp.inf) for n in range(nb)]
             q = qg[h, a, 0]
             g = qg[h, a, 1]
             scores = [dot(q, kv[h][ids[n], 0], NT) * scale + bias[n] for n in range(nb)]
@@ -195,7 +212,7 @@
             row = first + a
             index = jnp.int32(members * nb)
             for n in range(nb):
-                hit = (pattern[row, n] - first + members == j) & (live[row, n] > 0)
+                hit = (pattern[n, row] - first + members == j) & (live[n, row] > 0)
                 index = jnp.where(hit, a * nb + n, index)
             terms.append(index)
         return sum(slots[index, which] for index in terms)
@@ -208,7 +225,6 @@
             return carry
 
         lax.fori_loop(0, members, outer, 0)
-        z_start(z_back, h)
 
         def inner(j, carry):
             for which in range(2):
@@ -218,48 +234,70 @@
         lax.fori_loop(0, members, inner, 0)
 
     def finish(h):
-        z_wait_recv(z_back, h)
-
-        @pl.when(has_below)
-        def _():
-            own[h] += grecv[h, 1].astype(jnp.float32)
-
-        @pl.when(has_above)
-        def _():
-            own[h] += grecv[h, 0].astype(jnp.float32)
-
-        total[h] = own[h].astype(jnp.bfloat16)
-        x_back_start(h, (0, 1))
-
+        for k in outward:
+            tile = peers[k]
+            z_wait_recv(z_back, h, (k,))
+
+            @pl.when(has_below)
+            def _():
+                own[h, tile] += grecv[h, 1, tile].astype(jnp.float32)
+
+            @pl.when(has_above)
+            def _():
+                own[h, tile] += grecv[h, 0, tile].astype(jnp.float32)
+
+            total[h, tile] = own[h, tile].astype(jnp.bfloat16)
+            x_back_start(h, (0, 1), (k,))
+
+    everyone = tuple(range(members))
+    near, far = everyone[:2], everyone[2:]
+    outward = everyone[::-1]
+
+    table_copies = [
+        pltpu.make_async_copy(pattern_in, pattern, table_sem.at[0]),
+        pltpu.make_async_copy(live_in, live, table_sem.at[1]),
+    ]
+    for copy in table_copies:
+        copy.start()
     for h in range(heads):
-        for arr in range(4):
-            for off in range(members - 1):
-                x_in(h, arr, off).start()
-            x_own(h, arr).start()
+        for arrs in ((0, 1), (2, 3)):
+            for k in everyone:
+                for arr in arrs:
+                    if k == 0:
+                        x_own(h, arr).start()
+                    else:
+                        x_in(h, arr, k - 1).start()
 
     slots[members * nb] = jnp.zeros(slots.shape[1:], slots.dtype)
 
-    def feed(h):
-        x_in_wait(h, (0, 1))
-        z_start(z_in, h)
-
-    feed(0)
+    def feed(h, ks):
+        x_in_wait(h, (0, 1), ks)
+        z_start(z_in, h, ks)
+
+    def work(h):
+        x_in_wait(h, (2, 3), everyone)
+        z_wait_recv(z_in, h, everyone)
+        attend(h)
+        x_back_start(h, (2, 3), outward)
+        spread(h)
+
+    ahead = [(h, ks) for h in range(heads) for ks in (near, far)]
+    for h, ks in ahead[:5]:
+        feed(h, ks)
+    for copy in table_copies:
+        copy.wait()
     for h in range(heads):
-        if h + 1 < heads:
-            feed(h + 1)
-        x_in_wait(h, (2, 3))
-        z_wait_recv(z_in, h)
-        attend(h)
-        x_back_start(h, (2, 3))
-        spread(h)
-        if h >= 2:
-            finish(h - 2)
-    for h in range(max(heads - 2, 0), heads):
+        work(h)
+        if h == 0:
+            for item in ahead[5:]:
+                feed(*item)
+        z_start(z_back, h, outward)
+    for h in range(heads):
         finish(h)
 
     for h in range(heads):
-        z_wait_send(z_in, h)
-        z_wait_send(z_back, h)
+        z_wait_send(z_in, h, everyone)
+        z_wait_send(z_back, h, everyone)
         for arr in range(4):
             x_back_own(h, arr).wait()
             for off in range(members - 1):
@@ -268,18 +306,43 @@
                 x_back(h, arr, off).wait_recv()
 
 
+def place(*refs):
+    count = (len(refs) - 2) // 3
+    sources, outs, held = refs[:count], refs[count : 2 * count], refs[2 * count : 3 * count]
+    in_sem, out_sem = refs[-2:]
+    parts = 2
+    rows = sources[0].shape[0] // parts
+    pieces = [(i, part) for i in range(count) for part in range(parts)]
+
+    def load(i, part):
+        rng = pl.ds(part * rows, rows)
+        return pltpu.make_async_copy(sources[i].at[rng], held[i].at[rng], in_sem.at[i, part])
+
+    def store(i, part):
+        rng = pl.ds(part * rows, rows)
+        return pltpu.make_async_copy(held[i].at[rng], outs[i].at[rng], out_sem.at[i, part])
+
+    for piece in pieces:
+        load(*piece).start()
+    for piece in pieces:
+        load(*piece).wait()
+        store(*piece).start()
+    for piece in pieces:
+        store(*piece).wait()
+
+
 def body(members, layers, query, key_in, value, grad_out, pattern, live):
+    pattern, live = pattern.T, live.T
     tile = query.shape[0]
     heads = HEADS // members
-    nb = pattern.shape[1]
+    nb = pattern.shape[0]
     dma = pltpu.SemaphoreType.DMA
     bf16 = jnp.bfloat16
     block = (tile, HEAD_DIM)
-    return pl.pallas_call(
+    results = pl.pallas_call(
         functools.partial(kernel, members, layers),
         out_shape=[jax.ShapeDtypeStruct(query.shape, bf16)] * 4,
-        in_specs=[pl.BlockSpec(memory_space=pltpu.SMEM)] * 2
-        + [pl.BlockSpec(memory_space=pl.ANY)] * 4,
+        in_specs=[pl.BlockSpec(memory_space=pl.ANY)] * 6,
         out_specs=[pl.BlockSpec(memory_space=pl.ANY)] * 4,
         scratch_shapes=[
             pltpu.VMEM((heads, members, 2) + block, bf16),
@@ -289,13 +352,16 @@
             pltpu.VMEM((heads, 2, members, 2) + block, bf16),
             pltpu.VMEM((heads, 2, members, 2) + block, bf16),
             pltpu.VMEM((heads, members, 2) + block, bf16),
+            pltpu.SMEM(pattern.shape, jnp.int32),
+            pltpu.SMEM(live.shape, jnp.int32),
+            dma((2,)),
             dma((heads, 4, members - 1)),
             dma((heads, 4, members - 1)),
             dma((heads, 4)),
-            dma((heads, 2)),
-            dma((heads, 2)),
-            dma((heads, 2)),
-            dma((heads, 2)),
+            dma((heads, members, 2)),
+            dma((heads, members, 2)),
+            dma((heads, members, 2)),
+            dma((heads, members, 2)),
             dma((heads, 4, members - 1)),
             dma((heads, 4, members - 1)),
             dma((heads, 4)),
@@ -303,6 +369,14 @@
         + [pltpu.VMEM((3 * members, 2) + block, bf16)] * heads,
         compiler_params=pltpu.CompilerParams(collective_id=0, has_side_effects=True),
     )(pattern, live, query, key_in, value, grad_out)
+    count = len(results)
+    return pl.pallas_call(
+        place,
+        out_shape=[jax.ShapeDtypeStruct(query.shape, bf16)] * count,
+        in_specs=[pl.BlockSpec(memory_space=pl.ANY)] * count,
+        out_specs=[pl.BlockSpec(memory_space=pl.ANY)] * count,
+        scratch_shapes=[pltpu.VMEM(query.shape, bf16)] * count + [dma((count, 2))] * 2,
+    )(*results)
 
 
 def solution(mesh):

time: 99 us -> 80.7 us (0.82)
  Pallas kernels: 90.1 us -> 79.9 us
  local copies, waits for them, and re-layouts: 7.9 us -> 0 us
    pallas_call x1, Pallas kernels: 90.1 us -> 77.1 us  [body(): pl.pallas_call(functools.partial(kernel, members, layers), out_shape=[jax...]
    unnamed x14 -> x0, local copies, waits for them, and re-layouts: 7.9 us -> none
    pallas_call x0 -> x1, Pallas kernels: none -> 2.79 us  [body(): pl.pallas_call(place, out_shape=[jax.ShapeDtypeStruct(query.shape, bf16)]...]
where the time goes in v2:
time: 80.7 us; the launch traced here: 80.5 us
  Pallas kernels  79.9 us (99%)
    pallas_call x1, Pallas kernels, body(): pl.pallas_call(functools.partial(kernel, members, layers), out_shape=[jax...  77.1 us
    pallas_call x1, Pallas kernels, body(): pl.pallas_call(place, out_shape=[jax.ShapeDtypeStruct(query.shape, bf16)]...  2.79 us

profile of v2, /device:TPU:1, one launch (start us, length us, event | category | flops | bytes accessed | tf_op | source)
XLA Modules:
  0.0 80.5 jit_solution(7925507194473661034)
XLA Ops:
  0.6 77.1 %shard_map.93 = (bf16[256,1536]{1,0:T(8,128)(2,1)}, bf16[256,1536]{1,0:T(8,128)(2,1)}, bf16[256,1536]{1,0:T(8,128)(2,1)}, bf16[256,1536]{1,0:T(8,128)(2,1)}) custom-call(s32[3,16]{1,0:T(4,128)} %bitcast.2, s32[3,16]{1,0:T(4,128)} %bitcast.3, bf16[256,1536]{1,0:T(8,128)(2,1)} %query.1, bf16[256,1536]{1,0:T(8,128)(2,1)} %key_in.1, bf16[256,1536]{1,0:T(8,128)(2,1)} %value.1, ...), custom_call_target="tpu_custom_call" | custom-call | tf_op jit(solution)/shard_map/pallas_call | solution.py:342
  77.7 2.8 %shard_map.94 = (bf16[256,1536]{1,0:T(8,128)(2,1)}, bf16[256,1536]{1,0:T(8,128)(2,1)}, bf16[256,1536]{1,0:T(8,128)(2,1)}, bf16[256,1536]{1,0:T(8,128)(2,1)}) custom-call(bf16[256,1536]{1,0:T(8,128)(2,1)} %get-tuple-element.8.refs_0_, bf16[256,1536]{1,0:T(8,128)(2,1)} %get-tuple-element.9.refs_1_, bf16[256,1536]{1,0:T(8,128)(2,1)} %get-tuple-element.10.refs_2_, ...), custom_call_target="tpu_custom_call" | custom-call | tf_op jit(solution)/shard_map/pallas_call | solution.py:373

commit v3 on v2

--- a/solution.py
+++ b/solution.py
@@ -50,22 +50,6 @@
 
     def columns(owner, h):
         return pl.ds(pl.multiple_of((owner * heads + h) * HEAD_DIM, HEAD_DIM), HEAD_DIM)
-
-    barrier = pltpu.get_barrier_semaphore()
-    for p in partners:
-        pl.semaphore_signal(barrier, inc=1, device_id={"head": p}, device_id_type=MESH)
-
-    @pl.when(has_below)
-    def _():
-        pl.semaphore_signal(barrier, inc=1, device_id={"seq": below}, device_id_type=MESH)
-
-    @pl.when(has_above)
-    def _():
-        pl.semaphore_signal(barrier, inc=1, device_id={"seq": above}, device_id_type=MESH)
-
-    pl.semaphore_wait(
-        barrier, members - 1 + has_below.astype(jnp.int32) + has_above.astype(jnp.int32)
-    )
 
     sources = (key_in, value, query, grad_out)
 
@@ -252,27 +236,46 @@
     everyone = tuple(range(members))
     near, far = everyone[:2], everyone[2:]
     outward = everyone[::-1]
+    partner_ks = everyone[1:]
 
     table_copies = [
         pltpu.make_async_copy(pattern_in, pattern, table_sem.at[0]),
         pltpu.make_async_copy(live_in, live, table_sem.at[1]),
     ]
+    for h in range(heads):
+        for arr in range(4):
+            x_own(h, arr).start()
     for copy in table_copies:
         copy.start()
-    for h in range(heads):
-        for arrs in ((0, 1), (2, 3)):
-            for k in everyone:
-                for arr in arrs:
-                    if k == 0:
-                        x_own(h, arr).start()
-                    else:
-                        x_in(h, arr, k - 1).start()
-
-    slots[members * nb] = jnp.zeros(slots.shape[1:], slots.dtype)
+
+    barrier = pltpu.get_barrier_semaphore()
+    for p in partners:
+        pl.semaphore_signal(barrier, inc=1, device_id={"head": p}, device_id_type=MESH)
+
+    @pl.when(has_below)
+    def _():
+        pl.semaphore_signal(barrier, inc=1, device_id={"seq": below}, device_id_type=MESH)
+
+    @pl.when(has_above)
+    def _():
+        pl.semaphore_signal(barrier, inc=1, device_id={"seq": above}, device_id_type=MESH)
+
+    pl.semaphore_wait(
+        barrier, members - 1 + has_below.astype(jnp.int32) + has_above.astype(jnp.int32)
+    )
 
     def feed(h, ks):
         x_in_wait(h, (0, 1), ks)
         z_start(z_in, h, ks)
+
+    feed(0, near[:1])
+    for h in range(heads):
+        for arrs in ((0, 1), (2, 3)):
+            for k in partner_ks:
+                for arr in arrs:
+                    x_in(h, arr, k - 1).start()
+
+    slots[members * nb] = jnp.zeros(slots.shape[1:], slots.dtype)
 
     def work(h):
         x_in_wait(h, (2, 3), everyone)
@@ -282,6 +285,7 @@
         spread(h)
 
     ahead = [(h, ks) for h in range(heads) for ks in (near, far)]
+    ahead[0] = (0, near[1:])
     for h, ks in ahead[:5]:
         feed(h, ks)
     for copy in table_copies:

time: 80.7 us -> 80.7 us (level)
  no operation moved by 1% of the time
where the time goes in v3:
time: 80.7 us; the launch traced here: 80.5 us
  Pallas kernels  79.9 us (99%)
    pallas_call x1, Pallas kernels, body(): pl.pallas_call(functools.partial(kernel, members, layers), out_shape=[jax...  77.1 us
    pallas_call x1, Pallas kernels, body(): pl.pallas_call(place, out_shape=[jax.ShapeDtypeStruct(query.shape, bf16)]...  2.79 us

profile of v3, /device:TPU:1, one launch (start us, length us, event | category | flops | bytes accessed | tf_op | source)
XLA Modules:
  0.0 80.5 jit_solution(1396818931508623783)
XLA Ops:
  0.6 77.1 %shard_map.93 = (bf16[256,1536]{1,0:T(8,128)(2,1)}, bf16[256,1536]{1,0:T(8,128)(2,1)}, bf16[256,1536]{1,0:T(8,128)(2,1)}, bf16[256,1536]{1,0:T(8,128)(2,1)}) custom-call(s32[3,16]{1,0:T(4,128)} %bitcast.2, s32[3,16]{1,0:T(4,128)} %bitcast.3, bf16[256,1536]{1,0:T(8,128)(2,1)} %query.1, bf16[256,1536]{1,0:T(8,128)(2,1)} %key_in.1, bf16[256,1536]{1,0:T(8,128)(2,1)} %value.1, ...), custom_call_target="tpu_custom_call" | custom-call | tf_op jit(solution)/shard_map/pallas_call | solution.py:346
  77.8 2.8 %shard_map.94 = (bf16[256,1536]{1,0:T(8,128)(2,1)}, bf16[256,1536]{1,0:T(8,128)(2,1)}, bf16[256,1536]{1,0:T(8,128)(2,1)}, bf16[256,1536]{1,0:T(8,128)(2,1)}) custom-call(bf16[256,1536]{1,0:T(8,128)(2,1)} %get-tuple-element.8.refs_0_, bf16[256,1536]{1,0:T(8,128)(2,1)} %get-tuple-element.9.refs_1_, bf16[256,1536]{1,0:T(8,128)(2,1)} %get-tuple-element.10.refs_2_, ...), custom_call_target="tpu_custom_call" | custom-call | tf_op jit(solution)/shard_map/pallas_call | solution.py:377

commit v4 on v3

--- a/solution.py
+++ b/solution.py
@@ -311,28 +311,15 @@
 
 
 def place(*refs):
-    count = (len(refs) - 2) // 3
-    sources, outs, held = refs[:count], refs[count : 2 * count], refs[2 * count : 3 * count]
-    in_sem, out_sem = refs[-2:]
-    parts = 2
-    rows = sources[0].shape[0] // parts
-    pieces = [(i, part) for i in range(count) for part in range(parts)]
-
-    def load(i, part):
-        rng = pl.ds(part * rows, rows)
-        return pltpu.make_async_copy(sources[i].at[rng], held[i].at[rng], in_sem.at[i, part])
-
-    def store(i, part):
-        rng = pl.ds(part * rows, rows)
-        return pltpu.make_async_copy(held[i].at[rng], outs[i].at[rng], out_sem.at[i, part])
-
-    for piece in pieces:
-        load(*piece).start()
-    for piece in pieces:
-        load(*piece).wait()
-        store(*piece).start()
-    for piece in pieces:
-        store(*piece).wait()
+    count = len(refs) // 2
+    sems = refs[-1]
+    copies = [
+        pltpu.make_async_copy(refs[i], refs[count + i], sems.at[i]) for i in range(count)
+    ]
+    for copy in copies:
+        copy.start()
+    for copy in copies:
+        copy.wait()
 
 
 def body(members, layers, query, key_in, value, grad_out, pattern, live):
@@ -371,7 +358,7 @@
             dma((heads, 4)),
         ]
         + [pltpu.VMEM((3 * members, 2) + block, bf16)] * heads,
-        compiler_params=pltpu.CompilerParams(collective_id=0, has_side_effects=True),
+        compiler_params=pltpu.CompilerParams(collective_id=0, has_side_effects=True, vmem_limit_bytes=40 * 2**20),
     )(pattern, live, query, key_in, value, grad_out)
     count = len(results)
     return pl.pallas_call(
@@ -379,7 +366,8 @@
         out_shape=[jax.ShapeDtypeStruct(query.shape, bf16)] * count,
         in_specs=[pl.BlockSpec(memory_space=pl.ANY)] * count,
         out_specs=[pl.BlockSpec(memory_space=pl.ANY)] * count,
-        scratch_shapes=[pltpu.VMEM(query.shape, bf16)] * count + [dma((count, 2))] * 2,
+        scratch_shapes=[dma((count,))],
+        compiler_params=pltpu.CompilerParams(vmem_limit_bytes=8 * 2**20),
     )(*results)
 
 

time: 80.7 us -> 85.1 us (1.055)
  local copies, waits for them, and re-layouts: 0 us -> 5.89 us
  Pallas kernels: 79.9 us -> 78.2 us
    unnamed x0 -> x12, local copies, waits for them, and re-layouts: none -> 5.89 us
    pallas_call x1, Pallas kernels: 2.79 us -> 1.69 us  [body(): pl.pallas_call(place, out_shape=[jax.ShapeDtypeStruct(query.shape, bf16)]...]
where the time goes in v4:
time: 85.1 us; the launch traced here: 84.7 us
  Pallas kernels  78.2 us (92%)
  local copies, waits for them, and re-layouts  5.89 us (7%)
    pallas_call x1, Pallas kernels, body(): pl.pallas_call(functools.partial(kernel, members, layers), out_shape=[jax...  76.5 us
    unnamed x12, local copies, waits for them, and re-layouts  5.89 us

profile of v4, /device:TPU:1, one launch (start us, length us, event | category | flops | bytes accessed | tf_op | source)
XLA Modules:
  0.0 84.7 jit_solution(16343185233450379905)
XLA Ops:
  0.6 0.0 copy-start.4
  0.6 0.7 copy-done.4
  1.3 0.0 copy-start
  1.3 1.1 %copy-done = bf16[256,1536]{1,0:T(8,128)(2,1)S(1)} copy-done((bf16[256,1536]{1,0:T(8,128)(2,1)S(1)}, bf16[256,1536]{1,0:T(8,128)(2,1)}, u32[]{:S(2)}) %copy-start) | copy-done | bytes 786456
  2.4 0.0 copy-start.1
  2.5 1.1 %copy-done.1 = bf16[256,1536]{1,0:T(8,128)(2,1)S(1)} copy-done((bf16[256,1536]{1,0:T(8,128)(2,1)S(1)}, bf16[256,1536]{1,0:T(8,128)(2,1)}, u32[]{:S(2)}) %copy-start.1) | copy-done | bytes 786456
  3.6 0.0 copy-start.2
  3.6 1.1 %copy-done.2 = bf16[256,1536]{1,0:T(8,128)(2,1)S(1)} copy-done((bf16[256,1536]{1,0:T(8,128)(2,1)S(1)}, bf16[256,1536]{1,0:T(8,128)(2,1)}, u32[]{:S(2)}) %copy-start.2) | copy-done | bytes 786456
  4.7 0.0 copy-start.3
  4.7 1.1 %copy-done.3 = bf16[256,1536]{1,0:T(8,128)(2,1)S(1)} copy-done((bf16[256,1536]{1,0:T(8,128)(2,1)S(1)}, bf16[256,1536]{1,0:T(8,128)(2,1)}, u32[]{:S(2)}) %copy-start.3) | copy-done | bytes 786456
  5.8 0.0 copy-start.5
  5.9 0.7 copy-done.5
  6.5 76.5 %shard_map.93 = (bf16[256,1536]{1,0:T(8,128)(2,1)S(1)}, bf16[256,1536]{1,0:T(8,128)(2,1)S(1)}, bf16[256,1536]{1,0:T(8,128)(2,1)S(1)}, bf16[256,1536]{1,0:T(8,128)(2,1)S(1)}) custom-call(s32[3,16]{1,0:T(4,128)S(1)} %bitcast.2, s32[3,16]{1,0:T(4,128)S(1)} %bitcast.3, bf16[256,1536]{1,0:T(8,128)(2,1)S(1)} %copy-done, bf16[256,1536]{1,0:T(8,128)(2,1)S(1)} %copy-done.1, ...), custom_call_target="tpu_custom_call" | custom-call | tf_op jit(solution)/shard_map/pallas_call | solution.py:333
  83.1 1.7 %shard_map.94 = (bf16[256,1536]{1,0:T(8,128)(2,1)}, bf16[256,1536]{1,0:T(8,128)(2,1)}, bf16[256,1536]{1,0:T(8,128)(2,1)}, bf16[256,1536]{1,0:T(8,128)(2,1)}) custom-call(bf16[256,1536]{1,0:T(8,128)(2,1)S(1)} %get-tuple-element.8.refs_0_, bf16[256,1536]{1,0:T(8,128)(2,1)S(1)} %get-tuple-element.9.refs_1_, bf16[256,1536]{1,0:T(8,128)(2,1)S(1)} %get-tuple-element.10.refs_2_, ...), custom_call_target="tpu_custom_call" | custom-call | tf_op jit(solution)/shard_map/pallas_call | solution.py:364
Async XLA Ops:
  0.6 0.7 copy-start.4
  1.3 1.1 %copy-start = (bf16[256,1536]{1,0:T(8,128)(2,1)S(1)}, bf16[256,1536]{1,0:T(8,128)(2,1)}, u32[]{:S(2)}) copy-start(bf16[256,1536]{1,0:T(8,128)(2,1)} %query.1) | copy-start | bytes 2359300
  2.4 1.1 %copy-start.1 = (bf16[256,1536]{1,0:T(8,128)(2,1)S(1)}, bf16[256,1536]{1,0:T(8,128)(2,1)}, u32[]{:S(2)}) copy-start(bf16[256,1536]{1,0:T(8,128)(2,1)} %key_in.1) | copy-start | bytes 2359300
  3.6 1.1 %copy-start.2 = (bf16[256,1536]{1,0:T(8,128)(2,1)S(1)}, bf16[256,1536]{1,0:T(8,128)(2,1)}, u32[]{:S(2)}) copy-start(bf16[256,1536]{1,0:T(8,128)(2,1)} %value.1) | copy-start | bytes 2359300
  4.7 1.1 %copy-start.3 = (bf16[256,1536]{1,0:T(8,128)(2,1)S(1)}, bf16[256,1536]{1,0:T(8,128)(2,1)}, u32[]{:S(2)}) copy-start(bf16[256,1536]{1,0:T(8,128)(2,1)} %grad_out.1) | copy-start | bytes 2359300
  5.8 0.7 copy-start.5
